TPU v7x, 32 devices: a whole 2x2x4 slice. The times are simulated.
32 devices in a mesh: wide: 8 (over z, x), narrow: 4 (over y, core).
Axes of the slice: x: 2, y: 2, z: 4, core: 2. Of those that a mesh axis runs over, the one named last changes fastest.
Arguments:
- tokens: bfloat16 [4096, 2048], P(('wide', 'narrow')), may hold values from -6 to 6
- expert_ids: int32 [4096], P(('wide', 'narrow')), may hold values from 0 to 3, as said below
- route_weights: float32 [4096], P(('wide', 'narrow')), may hold values from 0.2 to 1
- out_grad: bfloat16 [4096, 2048], P(('wide', 'narrow')), may hold values from -0.796875 to 0.796875
- w_gate_up: bfloat16 [32, 2048, 256], P(('wide', 'narrow')), may hold values from -0.125 to 0.125
- w_down: bfloat16 [32, 128, 2048], P(('wide', 'narrow')), may hold values from -0.375 to 0.375
- second_moment: bfloat16 [32, 128, 2048], P(('wide', 'narrow')), may hold values from 0.0049743652 to 0.099609375
Outputs:
- grad_gate_up: bfloat16 [32, 2048, 256], P(('wide', 'narrow'))
- down_update: bfloat16 [32, 128, 2048], P(('wide', 'narrow'))
Inputs may be any that keep to these rules, and one draw needn't show every extreme that they name: `expert_ids`: values below 2 name the token's own group's experts, the others the next group's. Within the rows of one device no value appears more than 48 times; in every group of 4 devices along narrow one value appears exactly 48 times on every device of the group.
All inputs are finite; a program needn't handle non-finite values.
Results may differ from a plain program's by a relative error of at most 0.0066.
Values may be sent and summed in bfloat16 or wider, within the bound.
A program may use at most 64 MiB of HBM per device.

v0:
```python
import jax
import jax.numpy as jnp
from jax import lax
from jax.sharding import PartitionSpec as P

second_correction = 1.0 - 0.95**10


def passed_along(value, axis, steps):
    count = lax.axis_size(axis)
    pairs = [(source, (source + steps) % count) for source in range(count)]
    return lax.ppermute(value, axis, pairs)


def term_grads(rows_x, rows_d, weight_gu, weight_dn):
    width_half = weight_dn.shape[0]
    projected = jnp.dot(rows_x, weight_gu, preferred_element_type=jnp.float32)
    gate_pre = projected[:, :width_half]
    up_pre = projected[:, width_half:]
    logistic = jax.nn.sigmoid(gate_pre)
    swished = gate_pre * logistic
    hidden = (swished * up_pre).astype(jnp.bfloat16)
    down_grad = lax.dot_general(
        hidden, rows_d, (((0,), (0,)), ((), ())), preferred_element_type=jnp.float32
    )
    hidden_grad = lax.dot_general(
        rows_d, weight_dn, (((1,), (1,)), ((), ())), preferred_element_type=jnp.float32
    )
    gate_grad = hidden_grad * up_pre * logistic * (1.0 + gate_pre * (1.0 - logistic))
    up_grad = hidden_grad * swished
    pre_grads = jnp.concatenate([gate_grad, up_grad], axis=1).astype(jnp.bfloat16)
    proj_grad = lax.dot_general(
        rows_x, pre_grads, (((0,), (0,)), ((), ())), preferred_element_type=jnp.float32
    )
    return (proj_grad, down_grad)


def route_matrix(labels, groups, half_groups, capacity):
    experts_axis = jnp.arange(groups, dtype=jnp.int32)
    onehot = (labels[:, None] == experts_axis[None, :]).astype(jnp.int32)
    within = jnp.sum((jnp.cumsum(onehot, axis=0) - onehot) * onehot, axis=1)
    columns = jnp.arange(groups * 2 * capacity, dtype=jnp.int32)
    column_dest = columns // (2 * capacity)
    column_kind = columns // capacity % 2
    column_slot = columns % capacity
    matches = column_dest[None, :] // 2 == (labels % half_groups)[:, None]
    matches = matches & (column_kind[None, :] == (labels // half_groups)[:, None])
    matches = matches & (column_slot[None, :] == within[:, None])
    return matches.astype(jnp.bfloat16)


def place_rows(select, rows, groups):
    placed = lax.dot_general(
        select, rows, (((0,), (0,)), ((), ())), preferred_element_type=jnp.float32
    )
    return placed.astype(jnp.bfloat16).reshape(groups, -1, rows.shape[1])


def body(tokens, expert_ids, route_weights, out_grad, w_gate_up, w_down, second_moment):
    groups = lax.axis_size("narrow")
    half_groups = groups // 2
    tok_rows = tokens.shape[0]
    model_width = tokens.shape[1]
    capacity = 3 * tok_rows // (2 * groups)
    select = route_matrix(expert_ids, groups, half_groups, capacity)
    scaled = (route_weights[:, None] * out_grad.astype(jnp.float32)).astype(jnp.bfloat16)
    arrived = lax.all_to_all(
        place_rows(select, tokens, groups), "narrow", split_axis=0, concat_axis=0, tiled=True
    )
    arrived_grads = lax.all_to_all(
        place_rows(select, scaled, groups), "narrow", split_axis=0, concat_axis=0, tiled=True
    )
    own_x = arrived[:, :capacity].reshape(groups * capacity, model_width)
    own_d = arrived_grads[:, :capacity].reshape(groups * capacity, model_width)
    near_x = arrived[:, capacity:].reshape(groups * capacity, model_width)
    near_d = arrived_grads[:, capacity:].reshape(groups * capacity, model_width)
    weight_gu = w_gate_up[0]
    weight_dn = w_down[0]
    own_proj, own_down = term_grads(own_x, own_d, weight_gu, weight_dn)
    moved_x, moved_d = passed_along((near_x, near_d), "wide", 1)
    near_proj, near_down = term_grads(moved_x, moved_d, weight_gu, weight_dn)
    back_proj, back_down = lax.optimization_barrier(
        (near_proj.astype(jnp.bfloat16), near_down.astype(jnp.bfloat16))
    )
    total_proj = own_proj + back_proj.astype(jnp.float32)
    total_down = own_down + back_down.astype(jnp.float32)
    second = 0.95 * second_moment[0].astype(jnp.float32) + 0.05 * total_down * total_down
    update = total_down / (jnp.sqrt(second / second_correction) + 1e-08) + 0.1 * weight_dn.astype(
        jnp.float32
    )
    return (total_proj.astype(jnp.bfloat16)[None], update.astype(jnp.bfloat16)[None])


def solution(mesh):
    placed = (
        P(("wide", "narrow"), None),
        P(("wide", "narrow")),
        P(("wide", "narrow")),
        P(("wide", "narrow"), None),
        P(("wide", "narrow"), None, None),
        P(("wide", "narrow"), None, None),
        P(("wide", "narrow"), None, None),
    )
    return jax.shard_map(
        body,
        mesh=mesh,
        in_specs=placed,
        out_specs=(P(("wide", "narrow"), None, None), P(("wide", "narrow"), None, None)),
        check_vma=False,
    )
```

profile of v0, /device:TPU:0, one launch (start us, length us, event | category | flops | bytes accessed | tf_op | source)
XLA Modules:
  0.0 84.0 jit_solution(1018175137771871921)
XLA Ops:
  0.6 0.0 copy-start
  0.7 0.7 and_select_fusion.1
  1.4 0.7 fusion.27
  2.2 0.2 reduce_window_sum.11
  2.3 0.8 select_reduce_fusion
  3.2 2.9 %convolution_convert_fusion = bf16[384,2048]{1,0:T(8,128)(2,1)} fusion(bf16[128,2048]{1,0:T(8,128)(2,1)} %param.10, f32[128]{0:T(128)} %param.9, s32[384]{0:T(512)S(1)} %get-tuple-element.16, s32[384]{0:T(512)S(1)} %get-tuple-element.17, s32[384]{0:T(512)S(1)} %add_select_fusion.3, s32[128]{0:T(128)S(1)} %select_reduce_fusion, s32[128]{0:T(128)S(1)} %get-tuple-element.15, ...), kind=kOutput, calls=%fused_computation | convolution fusion | flops 203145216 | bytes 2103808 | tf_op jit(solution)/shard_map/dot_general | solution.py:53
  6.1 0.0 copy-start.1
  6.1 4.4 %all-to-all-start.1 = ((bf16[4,96,2048]{2,1,0:T(8,128)(2,1)}), bf16[4,96,2048]{2,1,0:T(8,128)(2,1)S(1)}, u32[]{:S(2)}, u32[]{:S(2)}) async-start(bf16[4,96,2048]{2,1,0:T(8,128)(2,1)} %bitcast.45), calls=%async_computation.1 | async-start | bytes 3145728 | tf_op jit(solution)/shard_map/all_to_all | solution.py:70
  10.5 0.0 copy-done.1
  10.5 1.9 %convolution_convert_fusion.1 = bf16[384,2048]{1,0:T(8,128)(2,1)} fusion(bf16[128,2048]{1,0:T(8,128)(2,1)S(1)} %copy-done.1, s32[384]{0:T(512)S(1)} %get-tuple-element.16, s32[384]{0:T(512)S(1)} %get-tuple-element.17, s32[384]{0:T(512)S(1)} %add_select_fusion.3, s32[128]{0:T(128)S(1)} %select_reduce_fusion, s32[128]{0:T(128)S(1)} %get-tuple-element.15, ...), kind=kOutput, calls=%fused_computation.1 | convolution fusion | flops 202358784 | bytes 2103296 | tf_op jit(solution)/shard_map/dot_general | solution.py:53
  12.4 18.2 %all-to-all-done.1 = bf16[4,96,2048]{2,1,0:T(8,128)(2,1)S(1)} async-done(((bf16[4,96,2048]{2,1,0:T(8,128)(2,1)}), bf16[4,96,2048]{2,1,0:T(8,128)(2,1)S(1)}, u32[]{:S(2)}, u32[]{:S(2)}) %all-to-all-start.1) | async-done | bytes 1572896 | tf_op jit(solution)/shard_map/all_to_all | solution.py:70
  30.5 4.3 %all-to-all-start = ((bf16[4,96,2048]{2,1,0:T(8,128)(2,1)}), bf16[4,96,2048]{2,1,0:T(8,128)(2,1)}, u32[]{:S(2)}, u32[]{:S(2)}) async-start(bf16[4,96,2048]{2,1,0:T(8,128)(2,1)} %bitcast.44), calls=%async_computation | async-start | bytes 3145728 | tf_op jit(solution)/shard_map/all_to_all | solution.py:67
  34.9 1.0 %fusion.44 = (bf16[4,48,2048]{2,1,0:T(8,128)(2,1)S(1)}, bf16[4,48,2048]{2,1,0:T(8,128)(2,1)}) fusion(bf16[4,96,2048]{2,1,0:T(8,128)(2,1)S(1)} %all-to-all-done.1), kind=kLoop, calls=%fused_computation.81 | loop fusion | bytes 3145728 | tf_op jit(solution)/shard_map/slice | solution.py:74
  35.9 2.2 %collective-permute-start.1 = (bf16[192,2048]{1,0:T(8,128)(2,1)}, bf16[192,2048]{1,0:T(8,128)(2,1)S(1)}, u32[]{:S(2)}, u32[]{:S(2)}) collective-permute-start(bf16[192,2048]{1,0:T(8,128)(2,1)} %bitcast.7), channel_id=1, source_target_pairs={{0,4},{4,8},{8,12},{12,16},{16,20},{20,24},{24,28},{28,0},{1,5},{5... | collective-permute-start | bytes 2359304 | tf_op jit(solution)/shard_map/ppermute | solution.py:12
  38.2 16.9 %all-to-all-done = bf16[4,96,2048]{2,1,0:T(8,128)(2,1)} async-done(((bf16[4,96,2048]{2,1,0:T(8,128)(2,1)}), bf16[4,96,2048]{2,1,0:T(8,128)(2,1)}, u32[]{:S(2)}, u32[]{:S(2)}) %all-to-all-start) | async-done | bytes 1572896 | tf_op jit(solution)/shard_map/all_to_all | solution.py:67
  55.0 1.5 %fusion.45 = (bf16[4,48,2048]{2,1,0:T(8,128)(2,1)S(1)}, bf16[4,48,2048]{2,1,0:T(8,128)(2,1)S(1)}) fusion(bf16[4,96,2048]{2,1,0:T(8,128)(2,1)} %all-to-all-done), kind=kLoop, calls=%fused_computation.82 | loop fusion | bytes 3145728 | tf_op jit(solution)/shard_map/slice | solution.py:75
  56.5 0.0 copy-start.2
  56.6 2.3 %collective-permute-start = (bf16[192,2048]{1,0:T(8,128)(2,1)S(1)}, bf16[192,2048]{1,0:T(8,128)(2,1)S(1)}, u32[]{:S(2)}, u32[]{:S(2)}) collective-permute-start(bf16[192,2048]{1,0:T(8,128)(2,1)S(1)} %bitcast.48), channel_id=1, source_target_pairs={{0,4},{4,8},{8,12},{12,16},{16,20},{20,24},{24,28},{28,0},{1,5},{5... | collective-permute-start | bytes 2359304 | tf_op jit(solution)/shard_map/ppermute | solution.py:12
  58.8 0.0 copy-done
  58.9 0.4 fusion.10
  59.2 0.0 copy-done.2
  59.3 0.4 multiply_convert_fusion.7
  59.7 0.3 fusion.28
  60.0 19.1 %collective-permute-done = bf16[192,2048]{1,0:T(8,128)(2,1)S(1)} collective-permute-done((bf16[192,2048]{1,0:T(8,128)(2,1)S(1)}, bf16[192,2048]{1,0:T(8,128)(2,1)S(1)}, u32[]{:S(2)}, u32[]{:S(2)}) %collective-permute-start) | collective-permute-done | bytes 786464 | tf_op jit(solution)/shard_map/ppermute | solution.py:12
  79.1 0.4 fusion.8
  79.5 0.0 collective-permute-done.1
  79.5 0.4 multiply_convert_fusion.5
  79.9 0.0 copy-start.3
  80.0 0.4 convolution_convert_fusion.3
  80.3 0.5 convolution_convert_fusion.2
  80.8 0.2 copy-done.3
  81.0 1.5 %fusion.18 = bf16[1,128,2048]{2,1,0:T(8,128)(2,1)} fusion(bf16[1,128,2048]{2,1,0:T(8,128)(2,1)S(1)} %copy-done.2, bf16[1,128,2048]{2,1,0:T(8,128)(2,1)S(1)} %copy-done.3, f32[128,2048]{1,0:T(8,128)S(1)} %fusion.28, bf16[128,2048]{1,0:T(8,128)(2,1)S(1)} %convolution_convert_fusion.3), kind=kLoop, calls=%fused_computation.25 | loop fusion | flops 3670016 | bytes 3145728 | tf_op jit(solution)/shard_map/broadcast_in_dim | solution.py:91
  82.5 1.5 %fusion.1 = bf16[1,2048,256]{2,1,0:T(8,128)(2,1)} fusion(bf16[192,2048]{1,0:T(8,128)(2,1)S(1)} %bitcast.43, bf16[2048,256]{1,0:T(8,128)(2,1)S(1)} %convolution_convert_fusion.2, bf16[192,128]{1,0:T(8,128)(2,1)S(1)} %get-tuple-element.11, bf16[192,128]{1,0:T(8,128)(2,1)S(1)} %get-tuple-element.10), kind=kOutput, calls=%fused_computation.5 | convolution fusion | flops 203096064 | bytes 2981888 | tf_op jit(solution)/shard_map/dot_general | solution.py:32
  (2 shorter events, 0.0 us)
Async XLA Ops:
  0.6 58.2 %copy-start = (bf16[1,2048,256]{2,1,0:T(8,128)(2,1)S(1)}, bf16[1,2048,256]{2,1,0:T(8,128)(2,1)}, u32[]{:S(2)}) copy-start(bf16[1,2048,256]{2,1,0:T(8,128)(2,1)} %param.11) | copy-start | bytes 3145732
  6.1 4.4 %copy-start.1 = (bf16[128,2048]{1,0:T(8,128)(2,1)S(1)}, bf16[128,2048]{1,0:T(8,128)(2,1)}, u32[]{:S(2)}) copy-start(bf16[128,2048]{1,0:T(8,128)(2,1)} %param.7) | copy-start | bytes 1572868
  6.1 24.4 %all-to-all-start.1 = ((bf16[4,96,2048]{2,1,0:T(8,128)(2,1)}), bf16[4,96,2048]{2,1,0:T(8,128)(2,1)S(1)}, u32[]{:S(2)}, u32[]{:S(2)}) async-start(bf16[4,96,2048]{2,1,0:T(8,128)(2,1)} %bitcast.45), calls=%async_computation.1 | async-start | bytes 3145728 | tf_op jit(solution)/shard_map/all_to_all | solution.py:70
  30.5 24.5 %all-to-all-start = ((bf16[4,96,2048]{2,1,0:T(8,128)(2,1)}), bf16[4,96,2048]{2,1,0:T(8,128)(2,1)}, u32[]{:S(2)}, u32[]{:S(2)}) async-start(bf16[4,96,2048]{2,1,0:T(8,128)(2,1)} %bitcast.44), calls=%async_computation | async-start | bytes 3145728 | tf_op jit(solution)/shard_map/all_to_all | solution.py:67
  35.9 43.6 %collective-permute-start.1 = (bf16[192,2048]{1,0:T(8,128)(2,1)}, bf16[192,2048]{1,0:T(8,128)(2,1)S(1)}, u32[]{:S(2)}, u32[]{:S(2)}) collective-permute-start(bf16[192,2048]{1,0:T(8,128)(2,1)} %bitcast.7), channel_id=1, source_target_pairs={{0,4},{4,8},{8,12},{12,16},{16,20},{20,24},{24,28},{28,0},{1,5},{5... | collective-permute-start | bytes 2359304 | tf_op jit(solution)/shard_map/ppermute | solution.py:12
  56.5 2.7 %copy-start.2 = (bf16[1,128,2048]{2,1,0:T(8,128)(2,1)S(1)}, bf16[1,128,2048]{2,1,0:T(8,128)(2,1)}, u32[]{:S(2)}) copy-start(bf16[1,128,2048]{2,1,0:T(8,128)(2,1)} %param.12) | copy-start | bytes 1572868
  56.6 22.6 %collective-permute-start = (bf16[192,2048]{1,0:T(8,128)(2,1)S(1)}, bf16[192,2048]{1,0:T(8,128)(2,1)S(1)}, u32[]{:S(2)}, u32[]{:S(2)}) collective-permute-start(bf16[192,2048]{1,0:T(8,128)(2,1)S(1)} %bitcast.48), channel_id=1, source_target_pairs={{0,4},{4,8},{8,12},{12,16},{16,20},{20,24},{24,28},{28,0},{1,5},{5... | collective-permute-start | bytes 2359304 | tf_op jit(solution)/shard_map/ppermute | solution.py:12
  79.9 1.0 %copy-start.3 = (bf16[1,128,2048]{2,1,0:T(8,128)(2,1)S(1)}, bf16[1,128,2048]{2,1,0:T(8,128)(2,1)}, u32[]{:S(2)}) copy-start(bf16[1,128,2048]{2,1,0:T(8,128)(2,1)} %param.13) | copy-start | bytes 1572868
where the time goes:
time: 84.4 us; the launch traced here: 84 us
  waiting for transfers between devices  54.1 us (64%)
  starting transfers between devices  13.3 us (16%)
  matrix products  9.03 us (11%)
  other arithmetic  4.06 us (5%)
  local copies, waits for them, and re-layouts  2.75 us (3%)
    ppermute x2, waiting for transfers between devices, passed_along(): return lax.ppermute(value, axis, pairs)  19.1 us
    all_to_all x1, waiting for transfers between devices, body(): lax.all_to_all(place_rows(select, scaled, groups), 'narrow', split_axis=0...  18.2 us
    all_to_all x1, waiting for transfers between devices, body(): lax.all_to_all(place_rows(select, tokens, groups), 'narrow', split_axis=0...  16.9 us
    dot_general x2, matrix products, place_rows(): lax.dot_general(select, rows, (((0,), (0,)), ((), ())), preferred_element...  4.78 us
    ppermute x2, starting transfers between devices, passed_along(): return lax.ppermute(value, axis, pairs)  4.53 us
    all_to_all x1, starting transfers between devices, body(): lax.all_to_all(place_rows(select, scaled, groups), 'narrow', split_axis=0...  4.4 us
    all_to_all x1, starting transfers between devices, body(): lax.all_to_all(place_rows(select, tokens, groups), 'narrow', split_axis=0...  4.34 us
    dot_general x2, matrix products, term_grads(): lax.dot_general(rows_x, pre_grads, (((0,), (0,)), ((), ())), preferred_el...  1.96 us
  transfers between devices with their start and end apart: 4, of which 3 were waited for; matrix products, arithmetic and copies ran while one was open for 7% of the time, Pallas kernels for 0%

commit v1 on v0

v1 whole, which is shorter than its diff:
```python
import functools

import jax
import jax.numpy as jnp
from jax import lax
from jax.experimental import pallas as pl
from jax.experimental.pallas import tpu as pltpu
from jax.sharding import PartitionSpec as P

second_correction = 1.0 - 0.95**10
bf16 = jnp.bfloat16
f32 = jnp.float32


def mm(a, b, dims):
    return lax.dot_general(a, b, (dims, ((), ())), preferred_element_type=f32)


def kernel(
    groups, wides, cap, slot, chunks,
    ids, rw, tok_hbm, og_hbm, wgu_hbm, wdn_hbm, sm_hbm,
    gout, uout,
    tok, og, wgu, wdn, sm, px, pd, rx, rd, pre, hid, acc_p, acc_d, gstage, ustage,
    in_sem, out_sem, sx, rxs, sd, rds, sc, rcs, fsx, frx, fsd, frd, fsc, frc,
):
    half = groups // 2
    width = tok.shape[1]
    hidden_units = wdn.shape[0]
    wide = lax.axis_index("wide")
    narrow = lax.axis_index("narrow")
    home = narrow // 2
    parity = lax.rem(narrow, 2)
    ahead = lax.rem(wide + 1, wides)
    behind = lax.rem(wide + wides - 1, wides)

    def device(w, n):
        return {"wide": w, "narrow": n}

    def expert_at(j):
        return lax.rem(home + j, half)

    sibling = device(wide, 2 * home + 1 - parity)

    order = [(0, 0), (1, 0)] + [(0, j) for j in range(1, half)] + [(1, j) for j in range(1, half)]
    early = 2 + (half - 1)
    late = half - 1
    remote_early = list(range(1, early))
    late_list = list(range(early, early + late))

    loads = []
    for i, (src, dst) in enumerate(
        ((tok_hbm, tok), (og_hbm, og), (wgu_hbm.at[0], wgu), (wdn_hbm.at[0], wdn), (sm_hbm.at[0], sm))
    ):
        copy = pltpu.make_async_copy(src, dst, in_sem.at[i])
        copy.start()
        loads.append(copy)

    barrier = pltpu.get_barrier_semaphore()
    partners = [sibling]
    for j in range(half):
        if j:
            partners.append(device(wide, 2 * expert_at(j) + parity))
        partners.append(device(ahead, 2 * expert_at(j) + parity))
        partners.append(device(behind, 2 * expert_at(j) + parity))
    for partner in partners:
        pl.semaphore_signal(barrier, inc=1, device_id=partner, device_id_type=pl.DeviceIdType.MESH)

    count = tok.shape[0]
    labels = ids[...]
    pad_groups = max(8, groups)
    onehot = (lax.broadcasted_iota(jnp.int32, (pad_groups, count), 0) == labels).astype(f32)
    before = (
        lax.broadcasted_iota(jnp.int32, (count, count), 0)
        < lax.broadcasted_iota(jnp.int32, (count, count), 1)
    ).astype(f32)
    counted = mm(onehot.astype(bf16), before.astype(bf16), ((1,), (0,)))
    within = jnp.sum(counted * onehot, axis=0, keepdims=True).astype(jnp.int32)
    weights = rw[...]
    slots = lax.broadcasted_iota(jnp.int32, (slot, count), 0)

    def select_of(b):
        kind, j = order[b]
        value = kind * half + expert_at(j)
        return jnp.logical_and(labels == value, slots == within)

    def rows(b, h):
        return pl.ds((2 * b + h) * slot, slot)

    def dest(b):
        kind, j = order[b]
        return device(ahead if kind else wide, 2 * expert_at(j) + parity)

    def remote(src, dst, s, r, dev):
        return pltpu.make_async_remote_copy(
            src_ref=src, dst_ref=dst, send_sem=s, recv_sem=r,
            device_id=dev, device_id_type=pl.DeviceIdType.MESH,
        )

    part = width // chunks

    def send_x(b):
        return remote(px.at[b], rx.at[rows(b, 0)], sx.at[b], rxs.at[b], dest(b))

    def send_d(b):
        return remote(pd.at[b], rd.at[rows(b, 0)], sd.at[b], rds.at[b], dest(b))

    def send_c(b, c):
        cols = pl.ds(c * part, part)
        i = (b - early) * chunks + c
        return remote(
            pd.at[b, :, cols], rd.at[rows(b, 0), cols], sc.at[i], rcs.at[i], dest(b)
        )

    def forward_x(b):
        return remote(rx.at[rows(b, 0)], rx.at[rows(b, 1)], fsx.at[b], frx.at[b], sibling)

    def forward_d(b):
        return remote(rd.at[rows(b, 0)], rd.at[rows(b, 1)], fsd.at[b], frd.at[b], sibling)

    def forward_c(b, c):
        cols = pl.ds(c * part, part)
        i = (b - early) * chunks + c
        return remote(
            rd.at[rows(b, 0), cols], rd.at[rows(b, 1), cols], fsc.at[i], frc.at[i], sibling
        )

    started = []

    def go(copy):
        copy.start()
        started.append(copy)

    def pack_x(b):
        return mm(select_of(b).astype(f32).astype(bf16), tok[...], ((1,), (0,))).astype(bf16)

    def pack_d(b):
        select = select_of(b)
        weight = jnp.sum(jnp.where(select, weights, 0.0), axis=1, keepdims=True)
        placed = mm(select.astype(f32).astype(bf16), og[...], ((1,), (0,)))
        return (weight * placed).astype(bf16)

    loads[0].wait()
    for b in remote_early:
        px[b] = pack_x(b)
    pl.semaphore_wait(barrier, len(partners))
    for b in remote_early:
        go(send_x(b))
    loads[1].wait()
    for b in remote_early:
        pd[b] = pack_d(b)
    for b in late_list:
        px[b] = pack_x(b)
    for b in remote_early:
        go(send_d(b))
    for b in late_list:
        go(send_x(b))
    for b in late_list:
        pd[b] = pack_d(b)
    rx[rows(0, 0), :] = pack_x(0)
    for b in late_list:
        for c in range(chunks):
            go(send_c(b, c))
    rd[rows(0, 0), :] = pack_d(0)
    go(forward_x(0))
    go(forward_d(0))
    loads[2].wait()
    loads[3].wait()

    def project(r):
        projected = mm(rx[r, :], wgu[...], ((1,), (0,)))
        gate_pre = projected[:, :hidden_units]
        up_pre = projected[:, hidden_units:]
        logistic = jax.nn.sigmoid(gate_pre)
        swished = gate_pre * logistic
        hid[r, :] = (swished * up_pre).astype(bf16)
        return up_pre * logistic * (1.0 + gate_pre * (1.0 - logistic)), swished

    def finish(r, hidden_grad, factors):
        pre[r, :] = jnp.concatenate(
            [hidden_grad * factors[0], hidden_grad * factors[1]], axis=1
        ).astype(bf16)

    for b in remote_early:
        send_x(b).wait_recv()
        go(forward_x(b))
    for b in remote_early:
        send_d(b).wait_recv()
        go(forward_d(b))
    for b in range(early):
        forward_x(b).wait_recv()
        forward_d(b).wait_recv()
    first = pl.ds(0, early * 2 * slot)
    finish(first, mm(rd[first, :], wdn[...], ((1,), (1,))), project(first))
    for i in range(width // 256):
        cols = pl.ds(i * 256, 256)
        acc_p[cols, :] = mm(rx[first, cols], pre[first, :], ((0,), (0,)))
        acc_d[:, cols] = mm(hid[first, :], rd[first, cols], ((0,), (0,)))

    for b in late_list:
        send_x(b).wait_recv()
        go(forward_x(b))
    for b in late_list:
        forward_x(b).wait_recv()
    last = pl.ds(early * 2 * slot, late * 2 * slot)
    factors = project(last)
    loads[4].wait()
    hidden_grad = jnp.zeros((late * 2 * slot, hidden_units), f32)
    outs = []

    def relay(c):
        for b in late_list:
            send_c(b, c).wait_recv()
            go(forward_c(b, c))

    relay(0)
    for c in range(chunks):
        if c + 1 < chunks:
            relay(c + 1)
        for b in late_list:
            forward_c(b, c).wait_recv()
        cols = pl.ds(c * part, part)
        hidden_grad = hidden_grad + mm(rd[last, cols], wdn[:, cols], ((1,), (1,)))
        if c == chunks - 1:
            finish(last, hidden_grad, factors)
            for i in range(width // 256):
                r = pl.ds(i * 256, 256)
                gstage[r, :] = (
                    acc_p[r, :] + mm(rx[last, r], pre[last, :], ((0,), (0,)))
                ).astype(bf16)
                copy = pltpu.make_async_copy(gstage.at[r], gout.at[0, r], out_sem.at[chunks + i])
                copy.start()
                outs.append(copy)
        total = acc_d[:, cols] + mm(hid[last, :], rd[last, cols], ((0,), (0,)))
        second = 0.95 * sm[:, cols].astype(f32) + 0.05 * total * total
        update = total / (jnp.sqrt(second / second_correction) + 1e-08)
        ustage[:, cols] = (update + 0.1 * wdn[:, cols].astype(f32)).astype(bf16)
        copy = pltpu.make_async_copy(ustage.at[:, cols], uout.at[0, :, cols], out_sem.at[c])
        copy.start()
        outs.append(copy)

    for copy in started:
        copy.wait_send()
    for copy in outs:
        copy.wait()


def body(tokens, expert_ids, route_weights, out_grad, w_gate_up, w_down, second_moment):
    groups = lax.axis_size("narrow")
    wides = lax.axis_size("wide")
    count, width = tokens.shape
    cap = 3 * count // (2 * groups)
    slot = -(-cap // 16) * 16
    chunks = 4
    columns = w_gate_up.shape[2]
    units = w_down.shape[1]
    all_rows = groups * 2 * slot
    late = groups // 2 - 1
    dma = pltpu.SemaphoreType.DMA
    any_spec = pl.BlockSpec(memory_space=pl.ANY)
    vmem_spec = pl.BlockSpec(memory_space=pltpu.VMEM)
    return pl.pallas_call(
        functools.partial(kernel, groups, wides, cap, slot, chunks),
        out_shape=(
            jax.ShapeDtypeStruct((1, width, columns), bf16),
            jax.ShapeDtypeStruct((1, units, width), bf16),
        ),
        in_specs=[vmem_spec, vmem_spec] + [any_spec] * 5,
        out_specs=(any_spec, any_spec),
        scratch_shapes=[
            pltpu.VMEM((count, width), bf16),
            pltpu.VMEM((count, width), bf16),
            pltpu.VMEM((width, columns), bf16),
            pltpu.VMEM((units, width), bf16),
            pltpu.VMEM((units, width), bf16),
            pltpu.VMEM((groups, slot, width), bf16),
            pltpu.VMEM((groups, slot, width), bf16),
            pltpu.VMEM((all_rows, width), bf16),
            pltpu.VMEM((all_rows, width), bf16),
            pltpu.VMEM((all_rows, columns), bf16),
            pltpu.VMEM((all_rows, units), bf16),
            pltpu.VMEM((width, columns), f32),
            pltpu.VMEM((units, width), f32),
            pltpu.VMEM((width, columns), bf16),
            pltpu.VMEM((units, width), bf16),
            dma((5,)),
            dma((chunks + width // 256,)),
            dma((groups,)), dma((groups,)), dma((groups,)), dma((groups,)),
            dma((late * chunks,)), dma((late * chunks,)),
            dma((groups,)), dma((groups,)), dma((groups,)), dma((groups,)),
            dma((late * chunks,)), dma((late * chunks,)),
        ],
        compiler_params=pltpu.CompilerParams(collective_id=0, has_side_effects=True),
    )(
        expert_ids.reshape(1, count), route_weights.reshape(1, count),
        tokens, out_grad, w_gate_up, w_down, second_moment,
    )


def solution(mesh):
    placed = (
        P(("wide", "narrow"), None),
        P(("wide", "narrow")),
        P(("wide", "narrow")),
        P(("wide", "narrow"), None),
        P(("wide", "narrow"), None, None),
        P(("wide", "narrow"), None, None),
        P(("wide", "narrow"), None, None),
    )
    return jax.shard_map(
        body,
        mesh=mesh,
        in_specs=placed,
        out_specs=(P(("wide", "narrow"), None, None), P(("wide", "narrow"), None, None)),
        check_vma=False,
    )
```

time: 84.4 us -> 33.6 us (0.40)
  waiting for transfers between devices: 54.1 us -> 0 us
  Pallas kernels: 0 us -> 29.6 us
  starting transfers between devices: 13.3 us -> 0 us
  matrix products: 9.03 us -> 0 us
  other arithmetic: 4.06 us -> 0 us
    all_to_all x2 -> x0, waiting for transfers between devices: 35 us -> none  [the longest x1 18.2 us: body(): lax.all_to_all(place_rows(select, scaled, groups), 'narrow', split_axis=0...]
    pallas_call x0 -> x1, Pallas kernels: none -> 29.6 us  [body(): pl.pallas_call(functools.partial(kernel, groups, wides, cap, slot, chunks...]
    ppermute x2 -> x0, waiting for transfers between devices: 19.1 us -> none  [passed_along(): return lax.ppermute(value, axis, pairs)]
    dot_general x10 -> x0, matrix products: 9.03 us -> none  [the longest x2 4.78 us: place_rows(): lax.dot_general(select, rows, (((0,), (0,)), ((), ())), preferred_element...]
    all_to_all x2 -> x0, starting transfers between devices: 8.73 us -> none  [the longest x1 4.4 us: body(): lax.all_to_all(place_rows(select, scaled, groups), 'narrow', split_axis=0...]
    ppermute x2 -> x0, starting transfers between devices: 4.53 us -> none  [passed_along(): return lax.ppermute(value, axis, pairs)]
    unnamed x8 -> x4, local copies, waits for them, and re-layouts: 0.19 us -> 3.12 us
    slice x2 -> x0, local copies, waits for them, and re-layouts: 2.56 us -> none  [the longest x1 1.54 us: body(): near_x = arrived[:, capacity:].reshape(groups * capacity, model_width)]
  transfers between devices with their start and end apart: 4 -> 0, of which waited for: 3 -> 0; matrix products, arithmetic and copies ran while one was open for 7% -> 0% of each run, Pallas kernels for 0% -> 0%
where the time goes in v1:
time: 33.6 us; the launch traced here: 33.4 us
  Pallas kernels  29.6 us (88%)
  local copies, waits for them, and re-layouts  3.12 us (9%)
  between operations  0.65 us (2%)
    pallas_call x1, Pallas kernels, body(): pl.pallas_call(functools.partial(kernel, groups, wides, cap, slot, chunks...  29.6 us
    unnamed x4, local copies, waits for them, and re-layouts  3.12 us

profile of v1, /device:TPU:0, one launch (start us, length us, event | category | flops | bytes accessed | tf_op | source)
XLA Modules:
  0.0 33.4 jit_solution(11620586048250449930)
XLA Ops:
  0.6 29.6 %shard_map.86 = (bf16[1,2048,256]{2,1,0:T(8,128)(2,1)}, bf16[1,128,2048]{2,1,0:T(8,128)(2,1)}) custom-call(s32[1,128]{1,0:T(1,128)} %bitcast.2, f32[1,128]{1,0:T(1,128)} %bitcast.3, bf16[128,2048]{1,0:T(8,128)(2,1)} %tok_hbm.1, bf16[128,2048]{1,0:T(8,128)(2,1)} %og_hbm.1, bf16[1,2048,256]{2,1,0:T(8,128)(2,1)} %wgu_hbm.1, bf16[1,128,2048]{2,1,0:T(8,128)(2,1)} %wdn_hbm.1, ...), custom_call_target="tpu_custom_call" | custom-call | tf_op jit(solution)/shard_map/pallas_call | solution.py:261
  30.3 0.0 copy-start
  30.3 2.3 %copy.11 = bf16[1,2048,256]{2,1,0:T(8,128)(2,1)} copy(bf16[1,2048,256]{2,1,0:T(8,128)(2,1)} %get-tuple-element.4) | data formatting | bytes 2097152
  32.6 0.0 copy-done
  32.6 0.8 %copy.12 = bf16[1,128,2048]{2,1,0:T(8,128)(2,1)} copy(bf16[1,128,2048]{2,1,0:T(8,128)(2,1)S(1)} %copy-done) | data formatting | bytes 1048576
Async XLA Ops:
  30.3 2.3 %copy-start = (bf16[1,128,2048]{2,1,0:T(8,128)(2,1)S(1)}, bf16[1,128,2048]{2,1,0:T(8,128)(2,1)}, u32[]{:S(2)}) copy-start(bf16[1,128,2048]{2,1,0:T(8,128)(2,1)} %get-tuple-element.5) | copy-start | bytes 1572868

commit v2 on v1

--- a/solution.py
+++ b/solution.py
@@ -10,6 +10,7 @@
 second_correction = 1.0 - 0.95**10
 bf16 = jnp.bfloat16
 f32 = jnp.float32
+LIMIT = 32 * 1024 * 1024
 
 
 def mm(a, b, dims):
@@ -19,9 +20,9 @@
 def kernel(
     groups, wides, cap, slot, chunks,
     ids, rw, tok_hbm, og_hbm, wgu_hbm, wdn_hbm, sm_hbm,
-    gout, uout,
-    tok, og, wgu, wdn, sm, px, pd, rx, rd, pre, hid, acc_p, acc_d, gstage, ustage,
-    in_sem, out_sem, sx, rxs, sd, rds, sc, rcs, fsx, frx, fsd, frd, fsc, frc,
+    acc_p, rows_last, pre_last, ustage,
+    tok, og, wgu, wdn, sm, px, pd, rx, rd, pre, hid, acc_d,
+    in_sem, sx, rxs, sd, rds, sc, rcs, fsx, frx, fsd, frd, fsc, frc,
 ):
     half = groups // 2
     width = tok.shape[1]
@@ -56,12 +57,9 @@
         loads.append(copy)
 
     barrier = pltpu.get_barrier_semaphore()
-    partners = [sibling]
-    for j in range(half):
-        if j:
-            partners.append(device(wide, 2 * expert_at(j) + parity))
-        partners.append(device(ahead, 2 * expert_at(j) + parity))
-        partners.append(device(behind, 2 * expert_at(j) + parity))
+    partners = [device(behind, 2 * expert_at(j) + parity) for j in range(half)]
+    partners += [device(wide, 2 * expert_at(j) + parity) for j in range(1, half)]
+    partners.append(sibling)
     for partner in partners:
         pl.semaphore_signal(barrier, inc=1, device_id=partner, device_id_type=pl.DeviceIdType.MESH)
 
@@ -175,8 +173,8 @@
         hid[r, :] = (swished * up_pre).astype(bf16)
         return up_pre * logistic * (1.0 + gate_pre * (1.0 - logistic)), swished
 
-    def finish(r, hidden_grad, factors):
-        pre[r, :] = jnp.concatenate(
+    def finish(target, r, hidden_grad, factors):
+        target[r, :] = jnp.concatenate(
             [hidden_grad * factors[0], hidden_grad * factors[1]], axis=1
         ).astype(bf16)
 
@@ -190,7 +188,7 @@
         forward_x(b).wait_recv()
         forward_d(b).wait_recv()
     first = pl.ds(0, early * 2 * slot)
-    finish(first, mm(rd[first, :], wdn[...], ((1,), (1,))), project(first))
+    finish(pre, first, mm(rd[first, :], wdn[...], ((1,), (1,))), project(first))
     for i in range(width // 256):
         cols = pl.ds(i * 256, 256)
         acc_p[cols, :] = mm(rx[first, cols], pre[first, :], ((0,), (0,)))
@@ -203,9 +201,9 @@
         forward_x(b).wait_recv()
     last = pl.ds(early * 2 * slot, late * 2 * slot)
     factors = project(last)
+    rows_last[...] = rx[last, :]
     loads[4].wait()
     hidden_grad = jnp.zeros((late * 2 * slot, hidden_units), f32)
-    outs = []
 
     def relay(c):
         for b in late_list:
@@ -220,26 +218,26 @@
             forward_c(b, c).wait_recv()
         cols = pl.ds(c * part, part)
         hidden_grad = hidden_grad + mm(rd[last, cols], wdn[:, cols], ((1,), (1,)))
-        if c == chunks - 1:
-            finish(last, hidden_grad, factors)
-            for i in range(width // 256):
-                r = pl.ds(i * 256, 256)
-                gstage[r, :] = (
-                    acc_p[r, :] + mm(rx[last, r], pre[last, :], ((0,), (0,)))
-                ).astype(bf16)
-                copy = pltpu.make_async_copy(gstage.at[r], gout.at[0, r], out_sem.at[chunks + i])
-                copy.start()
-                outs.append(copy)
         total = acc_d[:, cols] + mm(hid[last, :], rd[last, cols], ((0,), (0,)))
         second = 0.95 * sm[:, cols].astype(f32) + 0.05 * total * total
         update = total / (jnp.sqrt(second / second_correction) + 1e-08)
         ustage[:, cols] = (update + 0.1 * wdn[:, cols].astype(f32)).astype(bf16)
-        copy = pltpu.make_async_copy(ustage.at[:, cols], uout.at[0, :, cols], out_sem.at[c])
+
+    finish(pre_last, slice(None), hidden_grad, factors)
+    for copy in started:
+        copy.wait_send()
+
+
+def final_kernel(acc_p, rows_last, pre_last, update, gout, uout, gstage, out_sem):
+    tiles = acc_p.shape[0] // 256
+    outs = [pltpu.make_async_copy(update, uout.at[0], out_sem.at[tiles])]
+    outs[0].start()
+    for i in range(tiles):
+        r = pl.ds(i * 256, 256)
+        gstage[r, :] = (acc_p[r, :] + mm(rows_last[:, r], pre_last[...], ((0,), (0,)))).astype(bf16)
+        copy = pltpu.make_async_copy(gstage.at[r], gout.at[0, r], out_sem.at[i])
         copy.start()
         outs.append(copy)
-
-    for copy in started:
-        copy.wait_send()
     for copy in outs:
         copy.wait()
 
@@ -258,14 +256,17 @@
     dma = pltpu.SemaphoreType.DMA
     any_spec = pl.BlockSpec(memory_space=pl.ANY)
     vmem_spec = pl.BlockSpec(memory_space=pltpu.VMEM)
-    return pl.pallas_call(
+    last_rows = late * 2 * slot
+    held = pl.pallas_call(
         functools.partial(kernel, groups, wides, cap, slot, chunks),
         out_shape=(
-            jax.ShapeDtypeStruct((1, width, columns), bf16),
-            jax.ShapeDtypeStruct((1, units, width), bf16),
+            pltpu.VMEM((width, columns), f32),
+            pltpu.VMEM((last_rows, width), bf16),
+            pltpu.VMEM((last_rows, columns), bf16),
+            pltpu.VMEM((units, width), bf16),
         ),
-        in_specs=[vmem_spec, vmem_spec] + [any_spec] * 5,
-        out_specs=(any_spec, any_spec),
+        in_specs=[vmem_spec, vmem_spec] + [pl.BlockSpec(memory_space=pltpu.HBM)] * 5,
+        out_specs=(vmem_spec,) * 4,
         scratch_shapes=[
             pltpu.VMEM((count, width), bf16),
             pltpu.VMEM((count, width), bf16),
@@ -278,22 +279,31 @@
             pltpu.VMEM((all_rows, width), bf16),
             pltpu.VMEM((all_rows, columns), bf16),
             pltpu.VMEM((all_rows, units), bf16),
-            pltpu.VMEM((width, columns), f32),
             pltpu.VMEM((units, width), f32),
-            pltpu.VMEM((width, columns), bf16),
-            pltpu.VMEM((units, width), bf16),
             dma((5,)),
-            dma((chunks + width // 256,)),
             dma((groups,)), dma((groups,)), dma((groups,)), dma((groups,)),
             dma((late * chunks,)), dma((late * chunks,)),
             dma((groups,)), dma((groups,)), dma((groups,)), dma((groups,)),
             dma((late * chunks,)), dma((late * chunks,)),
         ],
-        compiler_params=pltpu.CompilerParams(collective_id=0, has_side_effects=True),
+        compiler_params=pltpu.CompilerParams(
+            collective_id=0, has_side_effects=True, vmem_limit_bytes=LIMIT
+        ),
     )(
         expert_ids.reshape(1, count), route_weights.reshape(1, count),
         tokens, out_grad, w_gate_up, w_down, second_moment,
     )
+    return pl.pallas_call(
+        final_kernel,
+        out_shape=(
+            jax.ShapeDtypeStruct((1, width, columns), bf16),
+            jax.ShapeDtypeStruct((1, units, width), bf16),
+        ),
+        in_specs=[vmem_spec] * 4,
+        out_specs=(any_spec, any_spec),
+        scratch_shapes=[pltpu.VMEM((width, columns), bf16), dma((width // 256 + 1,))],
+        compiler_params=pltpu.CompilerParams(vmem_limit_bytes=LIMIT),
+    )(*held)
 
 
 def solution(mesh):

time: 33.6 us -> 36.2 us (1.077)
  local copies, waits for them, and re-layouts: 3.12 us -> 6.69 us
  Pallas kernels: 29.6 us -> 28.5 us
    unnamed x4 -> x14, local copies, waits for them, and re-layouts: 3.12 us -> 6.69 us
    pallas_call x1, Pallas kernels: 29.6 us -> 27.2 us  [body(): pl.pallas_call(functools.partial(kernel, groups, wides, cap, slot, chunks...]
    pallas_call x0 -> x1, Pallas kernels: none -> 1.3 us  [body(): pl.pallas_call(final_kernel, out_shape=(jax.ShapeDtypeStruct((1, width, c...]
where the time goes in v2:
time: 36.2 us; the launch traced here: 35.8 us
  Pallas kernels  28.5 us (79%)
  local copies, waits for them, and re-layouts  6.69 us (18%)
  between operations  0.65 us (2%)
    pallas_call x1, Pallas kernels, body(): pl.pallas_call(functools.partial(kernel, groups, wides, cap, slot, chunks...  27.2 us
    unnamed x14, local copies, waits for them, and re-layouts  6.69 us
    pallas_call x1, Pallas kernels, body(): pl.pallas_call(final_kernel, out_shape=(jax.ShapeDtypeStruct((1, width, c...  1.3 us

profile of v2, /device:TPU:0, one launch (start us, length us, event | category | flops | bytes accessed | tf_op | source)
XLA Modules:
  0.0 35.8 jit_solution(15293178885276998418)
XLA Ops:
  0.6 0.0 copy-start
  0.6 1.2 %copy-done = bf16[1,2048,256]{2,1,0:T(8,128)(2,1)S(1)} copy-done((bf16[1,2048,256]{2,1,0:T(8,128)(2,1)S(1)}, bf16[1,2048,256]{2,1,0:T(8,128)(2,1)}, u32[]{:S(2)}) %copy-start) | copy-done | bytes 1048600
  1.9 0.0 copy-start.1
  1.9 1.0 %copy-done.1 = bf16[128,2048]{1,0:T(8,128)(2,1)S(1)} copy-done((bf16[128,2048]{1,0:T(8,128)(2,1)S(1)}, bf16[128,2048]{1,0:T(8,128)(2,1)}, u32[]{:S(2)}) %copy-start.1) | copy-done | bytes 524312
  2.9 0.0 copy-start.2
  2.9 1.0 %copy-done.2 = bf16[128,2048]{1,0:T(8,128)(2,1)S(1)} copy-done((bf16[128,2048]{1,0:T(8,128)(2,1)S(1)}, bf16[128,2048]{1,0:T(8,128)(2,1)}, u32[]{:S(2)}) %copy-start.2) | copy-done | bytes 524312
  3.9 0.0 copy-start.3
  3.9 1.0 %copy-done.3 = bf16[1,128,2048]{2,1,0:T(8,128)(2,1)S(1)} copy-done((bf16[1,128,2048]{2,1,0:T(8,128)(2,1)S(1)}, bf16[1,128,2048]{2,1,0:T(8,128)(2,1)}, u32[]{:S(2)}) %copy-start.3) | copy-done | bytes 524312
  5.0 0.0 copy-start.4
  5.0 1.0 %copy-done.4 = bf16[1,128,2048]{2,1,0:T(8,128)(2,1)S(1)} copy-done((bf16[1,128,2048]{2,1,0:T(8,128)(2,1)S(1)}, bf16[1,128,2048]{2,1,0:T(8,128)(2,1)}, u32[]{:S(2)}) %copy-start.4) | copy-done | bytes 524312
  6.0 0.0 copy-start.5
  6.0 0.7 %copy-done.5 = s32[128]{0:T(128)S(1)} copy-done((s32[128]{0:T(128)S(1)}, s32[128]{0:T(128)}, u32[]{:S(2)}) %copy-start.5) | copy-done | bytes 536
  6.7 0.0 copy-start.6
  6.7 0.7 %copy-done.6 = f32[128]{0:T(128)S(1)} copy-done((f32[128]{0:T(128)S(1)}, f32[128]{0:T(128)}, u32[]{:S(2)}) %copy-start.6) | copy-done | bytes 536
  7.3 27.2 %shard_map.86 = (f32[2048,256]{1,0:T(8,128)S(1)}, bf16[96,2048]{1,0:T(8,128)(2,1)S(1)}, bf16[96,256]{1,0:T(8,128)(2,1)S(1)}, bf16[128,2048]{1,0:T(8,128)(2,1)S(1)}) custom-call(s32[1,128]{1,0:T(1,128)S(1)} %bitcast.2, f32[1,128]{1,0:T(1,128)S(1)} %bitcast.3, bf16[128,2048]{1,0:T(8,128)(2,1)S(1)} %copy-done.1, bf16[128,2048]{1,0:T(8,128)(2,1)S(1)} %copy-done.2, ...), custom_call_target="tpu_custom_call" | custom-call | tf_op jit(solution)/shard_map/pallas_call | solution.py:260
  34.5 1.3 %shard_map.87 = (bf16[1,2048,256]{2,1,0:T(8,128)(2,1)}, bf16[1,128,2048]{2,1,0:T(8,128)(2,1)}) custom-call(f32[2048,256]{1,0:T(8,128)S(1)} %get-tuple-element.6.acc_p, bf16[96,2048]{1,0:T(8,128)(2,1)S(1)} %get-tuple-element.7.rows_last, bf16[96,256]{1,0:T(8,128)(2,1)S(1)} %get-tuple-element.8.pre_last, bf16[128,2048]{1,0:T(8,128)(2,1)S(1)} %get-tuple-element.9.update), custom_call_target="tpu_custom_call" | custom-call | tf_op jit(solution)/shard_map/pallas_call | solution.py:296
Async XLA Ops:
  0.6 1.2 %copy-start = (bf16[1,2048,256]{2,1,0:T(8,128)(2,1)S(1)}, bf16[1,2048,256]{2,1,0:T(8,128)(2,1)}, u32[]{:S(2)}) copy-start(bf16[1,2048,256]{2,1,0:T(8,128)(2,1)} %wgu_hbm.1) | copy-start | bytes 3145732
  1.9 1.0 %copy-start.1 = (bf16[128,2048]{1,0:T(8,128)(2,1)S(1)}, bf16[128,2048]{1,0:T(8,128)(2,1)}, u32[]{:S(2)}) copy-start(bf16[128,2048]{1,0:T(8,128)(2,1)} %tok_hbm.1) | copy-start | bytes 1572868
  2.9 1.0 %copy-start.2 = (bf16[128,2048]{1,0:T(8,128)(2,1)S(1)}, bf16[128,2048]{1,0:T(8,128)(2,1)}, u32[]{:S(2)}) copy-start(bf16[128,2048]{1,0:T(8,128)(2,1)} %og_hbm.1) | copy-start | bytes 1572868
  3.9 1.0 %copy-start.3 = (bf16[1,128,2048]{2,1,0:T(8,128)(2,1)S(1)}, bf16[1,128,2048]{2,1,0:T(8,128)(2,1)}, u32[]{:S(2)}) copy-start(bf16[1,128,2048]{2,1,0:T(8,128)(2,1)} %wdn_hbm.1) | copy-start | bytes 1572868
  5.0 1.0 %copy-start.4 = (bf16[1,128,2048]{2,1,0:T(8,128)(2,1)S(1)}, bf16[1,128,2048]{2,1,0:T(8,128)(2,1)}, u32[]{:S(2)}) copy-start(bf16[1,128,2048]{2,1,0:T(8,128)(2,1)} %sm_hbm.1) | copy-start | bytes 1572868
  6.0 0.7 %copy-start.5 = (s32[128]{0:T(128)S(1)}, s32[128]{0:T(128)}, u32[]{:S(2)}) copy-start(s32[128]{0:T(128)} %param.8) | copy-start | bytes 1540
  6.7 0.7 %copy-start.6 = (f32[128]{0:T(128)S(1)}, f32[128]{0:T(128)}, u32[]{:S(2)}) copy-start(f32[128]{0:T(128)} %param.9) | copy-start | bytes 1540

commit v3 on v2

--- a/solution.py
+++ b/solution.py
@@ -19,9 +19,9 @@
 
 def kernel(
     groups, wides, cap, slot, chunks,
-    ids, rw, tok_hbm, og_hbm, wgu_hbm, wdn_hbm, sm_hbm,
+    ids_hbm, rw_hbm, tok_hbm, og_hbm, wgu_hbm, wdn_hbm, sm_hbm,
     acc_p, rows_last, pre_last, ustage,
-    tok, og, wgu, wdn, sm, px, pd, rx, rd, pre, hid, acc_d,
+    ids, rw, tok, og, wgu, wdn, sm, px, pd, rx, rd, pre, hid, acc_d,
     in_sem, sx, rxs, sd, rds, sc, rcs, fsx, frx, fsd, frd, fsc, frc,
 ):
     half = groups // 2
@@ -50,11 +50,15 @@
 
     loads = []
     for i, (src, dst) in enumerate(
-        ((tok_hbm, tok), (og_hbm, og), (wgu_hbm.at[0], wgu), (wdn_hbm.at[0], wdn), (sm_hbm.at[0], sm))
+        (
+            (tok_hbm, tok), (og_hbm, og), (wgu_hbm.at[0], wgu), (wdn_hbm.at[0], wdn),
+            (sm_hbm.at[0], sm), (ids_hbm, ids), (rw_hbm, rw),
+        )
     ):
         copy = pltpu.make_async_copy(src, dst, in_sem.at[i])
-        copy.start()
         loads.append(copy)
+    for i in (5, 0, 6, 1, 2, 3, 4):
+        loads[i].start()
 
     barrier = pltpu.get_barrier_semaphore()
     partners = [device(behind, 2 * expert_at(j) + parity) for j in range(half)]
@@ -63,6 +67,8 @@
     for partner in partners:
         pl.semaphore_signal(barrier, inc=1, device_id=partner, device_id_type=pl.DeviceIdType.MESH)
 
+    loads[5].wait()
+    loads[6].wait()
     count = tok.shape[0]
     labels = ids[...]
     pad_groups = max(8, groups)
@@ -265,9 +271,11 @@
             pltpu.VMEM((last_rows, columns), bf16),
             pltpu.VMEM((units, width), bf16),
         ),
-        in_specs=[vmem_spec, vmem_spec] + [pl.BlockSpec(memory_space=pltpu.HBM)] * 5,
+        in_specs=[any_spec] * 7,
         out_specs=(vmem_spec,) * 4,
         scratch_shapes=[
+            pltpu.VMEM((1, count), jnp.int32),
+            pltpu.VMEM((1, count), f32),
             pltpu.VMEM((count, width), bf16),
             pltpu.VMEM((count, width), bf16),
             pltpu.VMEM((width, columns), bf16),
@@ -280,7 +288,7 @@
             pltpu.VMEM((all_rows, columns), bf16),
             pltpu.VMEM((all_rows, units), bf16),
             pltpu.VMEM((units, width), f32),
-            dma((5,)),
+            dma((7,)),
             dma((groups,)), dma((groups,)), dma((groups,)), dma((groups,)),
             dma((late * chunks,)), dma((late * chunks,)),
             dma((groups,)), dma((groups,)), dma((groups,)), dma((groups,)),
@@ -290,8 +298,13 @@
             collective_id=0, has_side_effects=True, vmem_limit_bytes=LIMIT
         ),
     )(
-        expert_ids.reshape(1, count), route_weights.reshape(1, count),
-        tokens, out_grad, w_gate_up, w_down, second_moment,
+        *(
+            pltpu.with_memory_space_constraint(value, pltpu.HBM)
+            for value in (
+                expert_ids.reshape(1, count), route_weights.reshape(1, count),
+                tokens, out_grad, w_gate_up, w_down, second_moment,
+            )
+        ),
     )
     return pl.pallas_call(
         final_kernel,

time: 36.2 us -> 29.9 us (0.83)
  local copies, waits for them, and re-layouts: 6.69 us -> 0 us
  Pallas kernels: 28.5 us -> 29.1 us
    unnamed x14 -> x0, local copies, waits for them, and re-layouts: 6.69 us -> none
    pallas_call x1, Pallas kernels: 27.2 us -> 27.8 us  [body(): pl.pallas_call(functools.partial(kernel, groups, wides, cap, slot, chunks...]
where the time goes in v3:
time: 29.9 us; the launch traced here: 29.8 us
  Pallas kernels  29.1 us (97%)
  between operations  0.64 us (2%)
    pallas_call x1, Pallas kernels, body(): pl.pallas_call(functools.partial(kernel, groups, wides, cap, slot, chunks...  27.8 us
    pallas_call x1, Pallas kernels, body(): pl.pallas_call(final_kernel, out_shape=(jax.ShapeDtypeStruct((1, width, c...  1.31 us

profile of v3, /device:TPU:0, one launch (start us, length us, event | category | flops | bytes accessed | tf_op | source)
XLA Modules:
  0.0 29.8 jit_solution(7748050021657491451)
XLA Ops:
  0.6 27.8 %shard_map.86 = (f32[2048,256]{1,0:T(8,128)S(1)}, bf16[96,2048]{1,0:T(8,128)(2,1)S(1)}, bf16[96,256]{1,0:T(8,128)(2,1)S(1)}, bf16[128,2048]{1,0:T(8,128)(2,1)S(1)}) custom-call(s32[1,128]{1,0:T(1,128)} %bitcast.2, f32[1,128]{1,0:T(1,128)} %bitcast.3, bf16[128,2048]{1,0:T(8,128)(2,1)} %tok_hbm.1, bf16[128,2048]{1,0:T(8,128)(2,1)} %og_hbm.1, ...), custom_call_target="tpu_custom_call" | custom-call | tf_op jit(solution)/shard_map/pallas_call | solution.py:266
  28.5 1.3 %shard_map.87 = (bf16[1,2048,256]{2,1,0:T(8,128)(2,1)}, bf16[1,128,2048]{2,1,0:T(8,128)(2,1)}) custom-call(f32[2048,256]{1,0:T(8,128)S(1)} %get-tuple-element.6.acc_p, bf16[96,2048]{1,0:T(8,128)(2,1)S(1)} %get-tuple-element.7.rows_last, bf16[96,256]{1,0:T(8,128)(2,1)S(1)} %get-tuple-element.8.pre_last, bf16[128,2048]{1,0:T(8,128)(2,1)S(1)} %get-tuple-element.9.update), custom_call_target="tpu_custom_call" | custom-call | tf_op jit(solution)/shard_map/pallas_call | solution.py:309

commit v4 on v3

--- a/solution.py
+++ b/solution.py
@@ -45,7 +45,7 @@
     order = [(0, 0), (1, 0)] + [(0, j) for j in range(1, half)] + [(1, j) for j in range(1, half)]
     early = 2 + (half - 1)
     late = half - 1
-    remote_early = list(range(1, early))
+    remote_early = list(range(2, early)) + [1]
     late_list = list(range(early, early + late))
 
     loads = []

time: 29.9 us -> 29.9 us (level)
  no operation moved by 1% of the time
where the time goes in v4:
time: 29.9 us; the launch traced here: 29.8 us
  Pallas kernels  29.1 us (97%)
  between operations  0.64 us (2%)
    pallas_call x1, Pallas kernels, body(): pl.pallas_call(functools.partial(kernel, groups, wides, cap, slot, chunks...  27.8 us
    pallas_call x1, Pallas kernels, body(): pl.pallas_call(final_kernel, out_shape=(jax.ShapeDtypeStruct((1, width, c...  1.3 us

profile of v4, /device:TPU:0, one launch (start us, length us, event | category | flops | bytes accessed | tf_op | source)
XLA Modules:
  0.0 29.8 jit_solution(9734368626778387471)
XLA Ops:
  0.6 27.8 %shard_map.86 = (f32[2048,256]{1,0:T(8,128)S(1)}, bf16[96,2048]{1,0:T(8,128)(2,1)S(1)}, bf16[96,256]{1,0:T(8,128)(2,1)S(1)}, bf16[128,2048]{1,0:T(8,128)(2,1)S(1)}) custom-call(s32[1,128]{1,0:T(1,128)} %bitcast.2, f32[1,128]{1,0:T(1,128)} %bitcast.3, bf16[128,2048]{1,0:T(8,128)(2,1)} %tok_hbm.1, bf16[128,2048]{1,0:T(8,128)(2,1)} %og_hbm.1, ...), custom_call_target="tpu_custom_call" | custom-call | tf_op jit(solution)/shard_map/pallas_call | solution.py:266
  28.5 1.3 %shard_map.87 = (bf16[1,2048,256]{2,1,0:T(8,128)(2,1)}, bf16[1,128,2048]{2,1,0:T(8,128)(2,1)}) custom-call(f32[2048,256]{1,0:T(8,128)S(1)} %get-tuple-element.6.acc_p, bf16[96,2048]{1,0:T(8,128)(2,1)S(1)} %get-tuple-element.7.rows_last, bf16[96,256]{1,0:T(8,128)(2,1)S(1)} %get-tuple-element.8.pre_last, bf16[128,2048]{1,0:T(8,128)(2,1)S(1)} %get-tuple-element.9.update), custom_call_target="tpu_custom_call" | custom-call | tf_op jit(solution)/shard_map/pallas_call | solution.py:309
